TPU v7x, 32 devices: a whole 2x2x4 slice. The times are simulated.
32 devices in a mesh: src: 8 (over y, x, core), tgt: 4 (over z).
Axes of the slice: x: 2, y: 2, z: 4, core: 2. Of those that a mesh axis runs over, the one named last changes fastest.
Arguments:
- src_coords: float32 [3, 49152], P(None, 'src'), may hold values from 0 to 1, as said below
- tgt_coords: float32 [3, 24576], P(None, 'tgt'), may hold values from 0 to 1
- src_scaling: float32 [32, 49152], P('tgt', 'src'), may hold values from 0.25 to 4
- src_mass: float32 [32, 49152], P('tgt', 'src'), may hold values from 0.25 to 4
- tgt_mass: float32 [32, 24576], P(None, 'tgt'), may hold values from 0.25 to 4
Outputs:
- new_src_scaling: float32 [32, 49152], P('tgt', 'src')
- tgt_scaling: float32 [32, 24576], P('src', 'tgt')
Inputs may be any that keep to these rules, and one draw needn't show every extreme that they name: `src_coords`: source points lie in the unit cube.
All inputs are finite; a program needn't handle non-finite values.
Results may differ from a plain program's by a relative error of at most 0.00036.
Values may be sent and summed in bfloat16 or wider, within the bound.
No kernel may reach another device: no remote copies, remote signals or barrier semaphores. Data moves between devices by JAX's collectives and lax.ppermute only.
A program may use at most 64 MiB of HBM per device.

v0:
```python
import jax
import jax.numpy as jnp
from jax import lax
from jax.sharding import PartitionSpec as P


def kernel_block(xb, yt):
    dist = (xb[0][:, None] - yt[0][None, :]) ** 2
    dist = dist + (xb[1][:, None] - yt[1][None, :]) ** 2
    dist = dist + (xb[2][:, None] - yt[2][None, :]) ** 2
    return (180.0 * jnp.exp(-100.0 * dist)).astype(jnp.bfloat16)


def on_device(src_coords, tgt_coords, src_scaling, src_mass, tgt_mass):
    src_pts = src_coords.shape[1]
    tgt_pts = tgt_coords.shape[1]
    weights = tgt_mass.shape[0]
    block = min(512, src_pts)
    count = src_pts // block
    xs_blocks = src_coords.reshape(3, count, block).transpose(1, 0, 2)
    src_low = lax.all_gather(src_scaling.astype(jnp.bfloat16), "tgt", axis=0, tiled=True)
    u_blocks = src_low.reshape(weights, count, block).transpose(1, 0, 2)

    def col_step(carry, items):
        xb, ub = items
        kern = kernel_block(xb, tgt_coords)
        return (carry + jnp.dot(ub, kern, preferred_element_type=jnp.float32), None)

    col_terms, _ = lax.scan(
        col_step, jnp.zeros((weights, tgt_pts), jnp.float32), (xs_blocks, u_blocks)
    )
    total_src = src_pts * lax.axis_size("src")
    share_rows = weights // lax.axis_size("src")
    col_full = lax.psum(col_terms, "src")
    scaling_full = tgt_mass / (col_full / total_src)
    tgt_scaling = lax.dynamic_slice_in_dim(
        scaling_full, lax.axis_index("src") * share_rows, share_rows, 0
    )
    tgt_low = scaling_full.astype(jnp.bfloat16)

    def row_step(xb):
        kern = kernel_block(xb, tgt_coords)
        return jnp.dot(tgt_low, kern.T, preferred_element_type=jnp.float32)

    rows = lax.map(row_step, xs_blocks)
    row_terms = rows.transpose(1, 0, 2).reshape(weights, src_pts)
    row_part = lax.psum_scatter(row_terms, "tgt", scatter_dimension=0, tiled=True)
    total_tgt = tgt_pts * lax.axis_size("tgt")
    new_src_scaling = src_mass / (row_part / total_tgt)
    return (new_src_scaling, tgt_scaling)


def solution(mesh):
    placed = (P(None, "src"), P(None, "tgt"), P("tgt", "src"), P("tgt", "src"), P(None, "tgt"))
    return jax.shard_map(
        on_device,
        mesh=mesh,
        in_specs=placed,
        out_specs=(P("tgt", "src"), P("src", "tgt")),
        check_vma=False,
    )
```

profile of v0, /device:TPU:0, one launch (start us, length us, event | category | flops | bytes accessed | tf_op | source)
XLA Modules:
  0.0 268.2 jit_solution(8683832820979956895)
XLA Ops:
  8.2 16.3 %all_gather.3 = bf16[32,6144]{1,0:T(8,128)(2,1)S(1)} all-gather(bf16[8,6144]{1,0:T(8,128)(2,1)S(1)} %convert_element_type.12), channel_id=1, replica_groups=mesh['src'=8,'tgt'=4] {'tgt'}, dimensions={0}, use_global_device_ids=true | all-gather | bytes 491520 | tf_op jit(solution)/shard_map/all_gather | solution.py:21
  25.3 76.9 %while.22 = (s32[]{:T(128)}, f32[32,6144]{1,0:T(8,128)S(1)}, bf16[12,32,512]{2,1,0:T(8,128)(2,1)S(1)}, f32[12,3,512]{2,1,0:T(4,128)}, f32[3,6144]{1,0:T(4,128)S(1)}, /*index=5*/s32[]{:T(128)}, s32[]{:T(128)}, s32[]{}, s32[]{}) while((s32[]{:T(128)}, f32[32,6144]{1,0:T(8,128)S(1)}, bf16[12,32,512]{2,1,0:T(8,128)(2,1)S(1)}, ...), condition=%wide.region_1.2_spmd.clone, body=%wide.region_0.1_spmd.clone.sunk | while | flops 236322816 | bytes 1845391 | solution.py:29
  26.2 5.5 %convolution_add_fusion.2 = f32[32,6144]{1,0:T(8,128)S(1)} fusion(f32[6144]{0:T(1024)S(1)} %bitcast.63, f32[512]{0:T(512)S(1)} %bitcast.70, f32[6144]{0:T(1024)S(1)} %bitcast.64, f32[512]{0:T(512)S(1)} %bitcast.69, f32[6144]{0:T(1024)S(1)} %bitcast.62, f32[512]{0:T(512)S(1)} %bitcast.68, f32[32,6144]{1,0:T(8,128)S(1)} %get-tuple-element.211, ...), kind=kOutput, calls=%fused_computation.10.clone.1 | convolution fusion | flops 236322816 | bytes 1685509 | tf_op jit(solution)/shard_map/while/body/eval_jaxpr/dot_general | solution.py:27
  32.6 5.5 %convolution_add_fusion.2 = f32[32,6144]{1,0:T(8,128)S(1)} fusion(f32[6144]{0:T(1024)S(1)} %bitcast.63, f32[512]{0:T(512)S(1)} %bitcast.70, f32[6144]{0:T(1024)S(1)} %bitcast.64, f32[512]{0:T(512)S(1)} %bitcast.69, f32[6144]{0:T(1024)S(1)} %bitcast.62, f32[512]{0:T(512)S(1)} %bitcast.68, f32[32,6144]{1,0:T(8,128)S(1)} %get-tuple-element.211, ...), kind=kOutput, calls=%fused_computation.10.clone.1 | convolution fusion | flops 236322816 | bytes 1685509 | tf_op jit(solution)/shard_map/while/body/eval_jaxpr/dot_general | solution.py:27
  39.0 5.5 %convolution_add_fusion.2 = f32[32,6144]{1,0:T(8,128)S(1)} fusion(f32[6144]{0:T(1024)S(1)} %bitcast.63, f32[512]{0:T(512)S(1)} %bitcast.70, f32[6144]{0:T(1024)S(1)} %bitcast.64, f32[512]{0:T(512)S(1)} %bitcast.69, f32[6144]{0:T(1024)S(1)} %bitcast.62, f32[512]{0:T(512)S(1)} %bitcast.68, f32[32,6144]{1,0:T(8,128)S(1)} %get-tuple-element.211, ...), kind=kOutput, calls=%fused_computation.10.clone.1 | convolution fusion | flops 236322816 | bytes 1685509 | tf_op jit(solution)/shard_map/while/body/eval_jaxpr/dot_general | solution.py:27
  45.4 5.5 %convolution_add_fusion.2 = f32[32,6144]{1,0:T(8,128)S(1)} fusion(f32[6144]{0:T(1024)S(1)} %bitcast.63, f32[512]{0:T(512)S(1)} %bitcast.70, f32[6144]{0:T(1024)S(1)} %bitcast.64, f32[512]{0:T(512)S(1)} %bitcast.69, f32[6144]{0:T(1024)S(1)} %bitcast.62, f32[512]{0:T(512)S(1)} %bitcast.68, f32[32,6144]{1,0:T(8,128)S(1)} %get-tuple-element.211, ...), kind=kOutput, calls=%fused_computation.10.clone.1 | convolution fusion | flops 236322816 | bytes 1685509 | tf_op jit(solution)/shard_map/while/body/eval_jaxpr/dot_general | solution.py:27
  51.8 5.5 %convolution_add_fusion.2 = f32[32,6144]{1,0:T(8,128)S(1)} fusion(f32[6144]{0:T(1024)S(1)} %bitcast.63, f32[512]{0:T(512)S(1)} %bitcast.70, f32[6144]{0:T(1024)S(1)} %bitcast.64, f32[512]{0:T(512)S(1)} %bitcast.69, f32[6144]{0:T(1024)S(1)} %bitcast.62, f32[512]{0:T(512)S(1)} %bitcast.68, f32[32,6144]{1,0:T(8,128)S(1)} %get-tuple-element.211, ...), kind=kOutput, calls=%fused_computation.10.clone.1 | convolution fusion | flops 236322816 | bytes 1685509 | tf_op jit(solution)/shard_map/while/body/eval_jaxpr/dot_general | solution.py:27
  58.3 5.5 %convolution_add_fusion.2 = f32[32,6144]{1,0:T(8,128)S(1)} fusion(f32[6144]{0:T(1024)S(1)} %bitcast.63, f32[512]{0:T(512)S(1)} %bitcast.70, f32[6144]{0:T(1024)S(1)} %bitcast.64, f32[512]{0:T(512)S(1)} %bitcast.69, f32[6144]{0:T(1024)S(1)} %bitcast.62, f32[512]{0:T(512)S(1)} %bitcast.68, f32[32,6144]{1,0:T(8,128)S(1)} %get-tuple-element.211, ...), kind=kOutput, calls=%fused_computation.10.clone.1 | convolution fusion | flops 236322816 | bytes 1685509 | tf_op jit(solution)/shard_map/while/body/eval_jaxpr/dot_general | solution.py:27
  64.7 5.5 %convolution_add_fusion.2 = f32[32,6144]{1,0:T(8,128)S(1)} fusion(f32[6144]{0:T(1024)S(1)} %bitcast.63, f32[512]{0:T(512)S(1)} %bitcast.70, f32[6144]{0:T(1024)S(1)} %bitcast.64, f32[512]{0:T(512)S(1)} %bitcast.69, f32[6144]{0:T(1024)S(1)} %bitcast.62, f32[512]{0:T(512)S(1)} %bitcast.68, f32[32,6144]{1,0:T(8,128)S(1)} %get-tuple-element.211, ...), kind=kOutput, calls=%fused_computation.10.clone.1 | convolution fusion | flops 236322816 | bytes 1685509 | tf_op jit(solution)/shard_map/while/body/eval_jaxpr/dot_general | solution.py:27
  71.1 5.5 %convolution_add_fusion.2 = f32[32,6144]{1,0:T(8,128)S(1)} fusion(f32[6144]{0:T(1024)S(1)} %bitcast.63, f32[512]{0:T(512)S(1)} %bitcast.70, f32[6144]{0:T(1024)S(1)} %bitcast.64, f32[512]{0:T(512)S(1)} %bitcast.69, f32[6144]{0:T(1024)S(1)} %bitcast.62, f32[512]{0:T(512)S(1)} %bitcast.68, f32[32,6144]{1,0:T(8,128)S(1)} %get-tuple-element.211, ...), kind=kOutput, calls=%fused_computation.10.clone.1 | convolution fusion | flops 236322816 | bytes 1685509 | tf_op jit(solution)/shard_map/while/body/eval_jaxpr/dot_general | solution.py:27
  77.5 5.5 %convolution_add_fusion.2 = f32[32,6144]{1,0:T(8,128)S(1)} fusion(f32[6144]{0:T(1024)S(1)} %bitcast.63, f32[512]{0:T(512)S(1)} %bitcast.70, f32[6144]{0:T(1024)S(1)} %bitcast.64, f32[512]{0:T(512)S(1)} %bitcast.69, f32[6144]{0:T(1024)S(1)} %bitcast.62, f32[512]{0:T(512)S(1)} %bitcast.68, f32[32,6144]{1,0:T(8,128)S(1)} %get-tuple-element.211, ...), kind=kOutput, calls=%fused_computation.10.clone.1 | convolution fusion | flops 236322816 | bytes 1685509 | tf_op jit(solution)/shard_map/while/body/eval_jaxpr/dot_general | solution.py:27
  83.9 5.5 %convolution_add_fusion.2 = f32[32,6144]{1,0:T(8,128)S(1)} fusion(f32[6144]{0:T(1024)S(1)} %bitcast.63, f32[512]{0:T(512)S(1)} %bitcast.70, f32[6144]{0:T(1024)S(1)} %bitcast.64, f32[512]{0:T(512)S(1)} %bitcast.69, f32[6144]{0:T(1024)S(1)} %bitcast.62, f32[512]{0:T(512)S(1)} %bitcast.68, f32[32,6144]{1,0:T(8,128)S(1)} %get-tuple-element.211, ...), kind=kOutput, calls=%fused_computation.10.clone.1 | convolution fusion | flops 236322816 | bytes 1685509 | tf_op jit(solution)/shard_map/while/body/eval_jaxpr/dot_general | solution.py:27
  90.3 5.5 %convolution_add_fusion.2 = f32[32,6144]{1,0:T(8,128)S(1)} fusion(f32[6144]{0:T(1024)S(1)} %bitcast.63, f32[512]{0:T(512)S(1)} %bitcast.70, f32[6144]{0:T(1024)S(1)} %bitcast.64, f32[512]{0:T(512)S(1)} %bitcast.69, f32[6144]{0:T(1024)S(1)} %bitcast.62, f32[512]{0:T(512)S(1)} %bitcast.68, f32[32,6144]{1,0:T(8,128)S(1)} %get-tuple-element.211, ...), kind=kOutput, calls=%fused_computation.10.clone.1 | convolution fusion | flops 236322816 | bytes 1685509 | tf_op jit(solution)/shard_map/while/body/eval_jaxpr/dot_general | solution.py:27
  96.7 5.5 %convolution_add_fusion.2 = f32[32,6144]{1,0:T(8,128)S(1)} fusion(f32[6144]{0:T(1024)S(1)} %bitcast.63, f32[512]{0:T(512)S(1)} %bitcast.70, f32[6144]{0:T(1024)S(1)} %bitcast.64, f32[512]{0:T(512)S(1)} %bitcast.69, f32[6144]{0:T(1024)S(1)} %bitcast.62, f32[512]{0:T(512)S(1)} %bitcast.68, f32[32,6144]{1,0:T(8,128)S(1)} %get-tuple-element.211, ...), kind=kOutput, calls=%fused_computation.10.clone.1 | convolution fusion | flops 236322816 | bytes 1685509 | tf_op jit(solution)/shard_map/while/body/eval_jaxpr/dot_general | solution.py:27
  103.4 57.3 %all-reduce.2.cloned.1.call-done = f32[32,6144]{1,0:T(8,128)} async-done(((f32[32,6144]{1,0:T(8,128)}), f32[32,6144]{1,0:T(8,128)}) %all-reduce.2.cloned.1.call-update) | async-done | bytes 786448 | tf_op jit(solution)/shard_map/psum | solution.py:34
  160.8 1.2 fusion.17
  162.0 74.1 %while.21 = (s32[]{:T(128)}, f32[12,32,512]{2,1,0:T(8,128)S(1)}, f32[12,3,512]{2,1,0:T(4,128)}, f32[3,6144]{1,0:T(4,128)S(1)}, bf16[32,6144]{1,0:T(8,128)(2,1)S(1)}, /*index=5*/s32[]{:T(128)}, s32[]{:T(128)}, s32[]{}, s32[]{}) while((s32[]{:T(128)}, f32[12,32,512]{2,1,0:T(8,128)S(1)}, f32[12,3,512]{2,1,0:T(4,128)}, f32[3,6144]{1,0:T(4,128)S(1)}, ...), condition=%wide.region_4.5_spmd, body=%wide.region_3.4_spmd.sunk | while | flops 235929600 | bytes 698501 | solution.py:45
  162.9 5.3 %fusion.28 = f32[12,32,512]{2,1,0:T(8,128)S(1)} fusion(f32[12,32,512]{2,1,0:T(8,128)S(1)} %get-tuple-element.238, s32[]{:T(128)} %get-tuple-element.237, bf16[32,6144]{1,0:T(8,128)(2,1)S(1)} %get-tuple-element.250, f32[6144]{0:T(1024)S(1)} %bitcast.66, f32[512]{0:T(512)S(1)} %bitcast.73, f32[6144]{0:T(1024)S(1)} %bitcast.67, f32[512]{0:T(512)S(1)} %bitcast.72, ...), kind=kOutput, calls=%fused_computation.3.clone.1 | convolution fusion | flops 235929600 | bytes 538628 | tf_op jit(solution)/shard_map/while/body/eval_jaxpr/dot_general | solution.py:43
  169.1 5.3 %fusion.28 = f32[12,32,512]{2,1,0:T(8,128)S(1)} fusion(f32[12,32,512]{2,1,0:T(8,128)S(1)} %get-tuple-element.238, s32[]{:T(128)} %get-tuple-element.237, bf16[32,6144]{1,0:T(8,128)(2,1)S(1)} %get-tuple-element.250, f32[6144]{0:T(1024)S(1)} %bitcast.66, f32[512]{0:T(512)S(1)} %bitcast.73, f32[6144]{0:T(1024)S(1)} %bitcast.67, f32[512]{0:T(512)S(1)} %bitcast.72, ...), kind=kOutput, calls=%fused_computation.3.clone.1 | convolution fusion | flops 235929600 | bytes 538628 | tf_op jit(solution)/shard_map/while/body/eval_jaxpr/dot_general | solution.py:43
  175.3 5.3 %fusion.28 = f32[12,32,512]{2,1,0:T(8,128)S(1)} fusion(f32[12,32,512]{2,1,0:T(8,128)S(1)} %get-tuple-element.238, s32[]{:T(128)} %get-tuple-element.237, bf16[32,6144]{1,0:T(8,128)(2,1)S(1)} %get-tuple-element.250, f32[6144]{0:T(1024)S(1)} %bitcast.66, f32[512]{0:T(512)S(1)} %bitcast.73, f32[6144]{0:T(1024)S(1)} %bitcast.67, f32[512]{0:T(512)S(1)} %bitcast.72, ...), kind=kOutput, calls=%fused_computation.3.clone.1 | convolution fusion | flops 235929600 | bytes 538628 | tf_op jit(solution)/shard_map/while/body/eval_jaxpr/dot_general | solution.py:43
  181.4 5.3 %fusion.28 = f32[12,32,512]{2,1,0:T(8,128)S(1)} fusion(f32[12,32,512]{2,1,0:T(8,128)S(1)} %get-tuple-element.238, s32[]{:T(128)} %get-tuple-element.237, bf16[32,6144]{1,0:T(8,128)(2,1)S(1)} %get-tuple-element.250, f32[6144]{0:T(1024)S(1)} %bitcast.66, f32[512]{0:T(512)S(1)} %bitcast.73, f32[6144]{0:T(1024)S(1)} %bitcast.67, f32[512]{0:T(512)S(1)} %bitcast.72, ...), kind=kOutput, calls=%fused_computation.3.clone.1 | convolution fusion | flops 235929600 | bytes 538628 | tf_op jit(solution)/shard_map/while/body/eval_jaxpr/dot_general | solution.py:43
  187.6 5.3 %fusion.28 = f32[12,32,512]{2,1,0:T(8,128)S(1)} fusion(f32[12,32,512]{2,1,0:T(8,128)S(1)} %get-tuple-element.238, s32[]{:T(128)} %get-tuple-element.237, bf16[32,6144]{1,0:T(8,128)(2,1)S(1)} %get-tuple-element.250, f32[6144]{0:T(1024)S(1)} %bitcast.66, f32[512]{0:T(512)S(1)} %bitcast.73, f32[6144]{0:T(1024)S(1)} %bitcast.67, f32[512]{0:T(512)S(1)} %bitcast.72, ...), kind=kOutput, calls=%fused_computation.3.clone.1 | convolution fusion | flops 235929600 | bytes 538628 | tf_op jit(solution)/shard_map/while/body/eval_jaxpr/dot_general | solution.py:43
  193.8 5.3 %fusion.28 = f32[12,32,512]{2,1,0:T(8,128)S(1)} fusion(f32[12,32,512]{2,1,0:T(8,128)S(1)} %get-tuple-element.238, s32[]{:T(128)} %get-tuple-element.237, bf16[32,6144]{1,0:T(8,128)(2,1)S(1)} %get-tuple-element.250, f32[6144]{0:T(1024)S(1)} %bitcast.66, f32[512]{0:T(512)S(1)} %bitcast.73, f32[6144]{0:T(1024)S(1)} %bitcast.67, f32[512]{0:T(512)S(1)} %bitcast.72, ...), kind=kOutput, calls=%fused_computation.3.clone.1 | convolution fusion | flops 235929600 | bytes 538628 | tf_op jit(solution)/shard_map/while/body/eval_jaxpr/dot_general | solution.py:43
  199.9 5.3 %fusion.28 = f32[12,32,512]{2,1,0:T(8,128)S(1)} fusion(f32[12,32,512]{2,1,0:T(8,128)S(1)} %get-tuple-element.238, s32[]{:T(128)} %get-tuple-element.237, bf16[32,6144]{1,0:T(8,128)(2,1)S(1)} %get-tuple-element.250, f32[6144]{0:T(1024)S(1)} %bitcast.66, f32[512]{0:T(512)S(1)} %bitcast.73, f32[6144]{0:T(1024)S(1)} %bitcast.67, f32[512]{0:T(512)S(1)} %bitcast.72, ...), kind=kOutput, calls=%fused_computation.3.clone.1 | convolution fusion | flops 235929600 | bytes 538628 | tf_op jit(solution)/shard_map/while/body/eval_jaxpr/dot_general | solution.py:43
  206.1 5.3 %fusion.28 = f32[12,32,512]{2,1,0:T(8,128)S(1)} fusion(f32[12,32,512]{2,1,0:T(8,128)S(1)} %get-tuple-element.238, s32[]{:T(128)} %get-tuple-element.237, bf16[32,6144]{1,0:T(8,128)(2,1)S(1)} %get-tuple-element.250, f32[6144]{0:T(1024)S(1)} %bitcast.66, f32[512]{0:T(512)S(1)} %bitcast.73, f32[6144]{0:T(1024)S(1)} %bitcast.67, f32[512]{0:T(512)S(1)} %bitcast.72, ...), kind=kOutput, calls=%fused_computation.3.clone.1 | convolution fusion | flops 235929600 | bytes 538628 | tf_op jit(solution)/shard_map/while/body/eval_jaxpr/dot_general | solution.py:43
  212.3 5.3 %fusion.28 = f32[12,32,512]{2,1,0:T(8,128)S(1)} fusion(f32[12,32,512]{2,1,0:T(8,128)S(1)} %get-tuple-element.238, s32[]{:T(128)} %get-tuple-element.237, bf16[32,6144]{1,0:T(8,128)(2,1)S(1)} %get-tuple-element.250, f32[6144]{0:T(1024)S(1)} %bitcast.66, f32[512]{0:T(512)S(1)} %bitcast.73, f32[6144]{0:T(1024)S(1)} %bitcast.67, f32[512]{0:T(512)S(1)} %bitcast.72, ...), kind=kOutput, calls=%fused_computation.3.clone.1 | convolution fusion | flops 235929600 | bytes 538628 | tf_op jit(solution)/shard_map/while/body/eval_jaxpr/dot_general | solution.py:43
  218.5 5.3 %fusion.28 = f32[12,32,512]{2,1,0:T(8,128)S(1)} fusion(f32[12,32,512]{2,1,0:T(8,128)S(1)} %get-tuple-element.238, s32[]{:T(128)} %get-tuple-element.237, bf16[32,6144]{1,0:T(8,128)(2,1)S(1)} %get-tuple-element.250, f32[6144]{0:T(1024)S(1)} %bitcast.66, f32[512]{0:T(512)S(1)} %bitcast.73, f32[6144]{0:T(1024)S(1)} %bitcast.67, f32[512]{0:T(512)S(1)} %bitcast.72, ...), kind=kOutput, calls=%fused_computation.3.clone.1 | convolution fusion | flops 235929600 | bytes 538628 | tf_op jit(solution)/shard_map/while/body/eval_jaxpr/dot_general | solution.py:43
  224.6 5.3 %fusion.28 = f32[12,32,512]{2,1,0:T(8,128)S(1)} fusion(f32[12,32,512]{2,1,0:T(8,128)S(1)} %get-tuple-element.238, s32[]{:T(128)} %get-tuple-element.237, bf16[32,6144]{1,0:T(8,128)(2,1)S(1)} %get-tuple-element.250, f32[6144]{0:T(1024)S(1)} %bitcast.66, f32[512]{0:T(512)S(1)} %bitcast.73, f32[6144]{0:T(1024)S(1)} %bitcast.67, f32[512]{0:T(512)S(1)} %bitcast.72, ...), kind=kOutput, calls=%fused_computation.3.clone.1 | convolution fusion | flops 235929600 | bytes 538628 | tf_op jit(solution)/shard_map/while/body/eval_jaxpr/dot_general | solution.py:43
  230.8 5.3 %fusion.28 = f32[12,32,512]{2,1,0:T(8,128)S(1)} fusion(f32[12,32,512]{2,1,0:T(8,128)S(1)} %get-tuple-element.238, s32[]{:T(128)} %get-tuple-element.237, bf16[32,6144]{1,0:T(8,128)(2,1)S(1)} %get-tuple-element.250, f32[6144]{0:T(1024)S(1)} %bitcast.66, f32[512]{0:T(512)S(1)} %bitcast.73, f32[6144]{0:T(1024)S(1)} %bitcast.67, f32[512]{0:T(512)S(1)} %bitcast.72, ...), kind=kOutput, calls=%fused_computation.3.clone.1 | convolution fusion | flops 235929600 | bytes 538628 | tf_op jit(solution)/shard_map/while/body/eval_jaxpr/dot_general | solution.py:43
  236.1 1.0 copy.10
  237.8 22.0 %reduce-scatter.2.cloned.1.call-done = f32[8,6144]{1,0:T(8,128)} async-done(((f32[32,6144]{1,0:T(8,128)}), f32[8,6144]{1,0:T(8,128)}) %reduce-scatter.2.cloned.1.call-update) | async-done | bytes 196624 | tf_op jit(solution)/shard_map/reduce_scatter | solution.py:47
  259.7 1.6 multiply_divide_fusion.1
  (66 shorter events, 24.7 us)
Async XLA Ops:
  7.2 153.6 %all-reduce.2.cloned.1.call-start = ((), (), s32[]{:S(2)}) async-start(), calls=%async_computation.1 | async-start | bytes 1572864 | tf_op jit(solution)/shard_map/psum | solution.py:34
  24.4 0.9 copy-start
  102.3 0.9 copy-start.1
  102.3 58.5 %copy-start.2 = (f32[32,6144]{1,0:T(8,128)S(1)}, f32[32,6144]{1,0:T(8,128)}, u32[]{:S(2)}) copy-start(f32[32,6144]{1,0:T(8,128)} %param.13) | copy-start | bytes 2359300
  103.2 156.5 %reduce-scatter.2.cloned.1.call-start = ((), (), s32[]{:S(2)}) async-start(), calls=%async_computation.2 | async-start | bytes 983040 | tf_op jit(solution)/shard_map/reduce_scatter | solution.py:47
  237.1 22.7 %copy-start.3 = (f32[8,6144]{1,0:T(8,128)S(1)}, f32[8,6144]{1,0:T(8,128)}, u32[]{:S(2)}) copy-start(f32[8,6144]{1,0:T(8,128)} %param.12) | copy-start | bytes 589828
Sparse Core Ops, SparseCore 0:
  103.3 57.4 all-reduce.1
  237.2 22.4 reduce-scatter.1
where the time goes:
time: 270 us; the launch traced here: 268 us
  matrix products  130 us (48%)
  waiting for transfers between devices  79.3 us (29%)
  local copies, waits for them, and re-layouts  24.4 us (9%)
  blocking collectives  16.3 us (6%)
  between operations  14.1 us (5%)
  other arithmetic  3.82 us (1%)
    dot_general x12, matrix products, col_step(): return (carry + jnp.dot(ub, kern, preferred_element_type=jnp.float32), None)  66.1 us
    dot_general x12, matrix products, row_step(): return jnp.dot(tgt_low, kern.T, preferred_element_type=jnp.float32)  63.5 us
    psum x1, waiting for transfers between devices, on_device(): col_full = lax.psum(col_terms, 'src')  57.3 us
    reduce_scatter x1, waiting for transfers between devices, on_device(): lax.psum_scatter(row_terms, 'tgt', scatter_dimension=0, tiled=True)  22 us
    slice x48, local copies, waits for them, and re-layouts, kernel_block(): dist = (xb[0][:, None] - yt[0][None, :]) ** 2  21 us
    all_gather x1, blocking collectives, on_device(): lax.all_gather(src_scaling.astype(jnp.bfloat16), 'tgt', axis=0, tiled=True)  16.3 us
  transfers between devices with their start and end apart: 2, of which 2 were waited for; matrix products, arithmetic and copies ran while one was open for 0% of the time, Pallas kernels for 0%

commit v1 on v0

--- a/solution.py
+++ b/solution.py
@@ -31,7 +31,8 @@
     )
     total_src = src_pts * lax.axis_size("src")
     share_rows = weights // lax.axis_size("src")
-    col_full = lax.psum(col_terms, "src")
+    parts = lax.all_gather(col_terms, "src")
+    col_full = jnp.sum(parts, axis=0)
     scaling_full = tgt_mass / (col_full / total_src)
     tgt_scaling = lax.dynamic_slice_in_dim(
         scaling_full, lax.axis_index("src") * share_rows, share_rows, 0

time: 270 us -> 288 us (1.067)
  local copies, waits for them, and re-layouts: 24.4 us -> 36.7 us
  matrix products: 130 us -> 142 us
  waiting for transfers between devices: 79.3 us -> 69.8 us
    psum x1 -> x0, waiting for transfers between devices: 57.3 us -> none  [on_device(): col_full = lax.psum(col_terms, 'src')]
    all_gather x0 -> x1, waiting for transfers between devices: none -> 47.1 us  [on_device(): parts = lax.all_gather(col_terms, 'src')]
    slice x48, local copies, waits for them, and re-layouts: 21 us -> 33.7 us  [kernel_block(): dist = (xb[0][:, None] - yt[0][None, :]) ** 2]
    dot_general x12, matrix products: 63.5 us -> 75.4 us  [row_step(): return jnp.dot(tgt_low, kern.T, preferred_element_type=jnp.float32)]
    reduce_sum x0 -> x1, other arithmetic: none -> 3.18 us  [on_device(): col_full = jnp.sum(parts, axis=0)]
where the time goes in v1:
time: 288 us; the launch traced here: 286 us
  matrix products  142 us (49%)
  waiting for transfers between devices  69.8 us (24%)
  local copies, waits for them, and re-layouts  36.7 us (13%)
  blocking collectives  16.3 us (6%)
  between operations  14.1 us (5%)
  other arithmetic  6.61 us (2%)
    dot_general x12, matrix products, row_step(): return jnp.dot(tgt_low, kern.T, preferred_element_type=jnp.float32)  75.4 us
    dot_general x12, matrix products, col_step(): return (carry + jnp.dot(ub, kern, preferred_element_type=jnp.float32), None)  66.1 us
    all_gather x1, waiting for transfers between devices, on_device(): parts = lax.all_gather(col_terms, 'src')  47.1 us
    slice x48, local copies, waits for them, and re-layouts, kernel_block(): dist = (xb[0][:, None] - yt[0][None, :]) ** 2  33.7 us
    reduce_scatter x1, waiting for transfers between devices, on_device(): lax.psum_scatter(row_terms, 'tgt', scatter_dimension=0, tiled=True)  22.7 us
    all_gather x1, blocking collectives, on_device(): lax.all_gather(src_scaling.astype(jnp.bfloat16), 'tgt', axis=0, tiled=True)  16.3 us
  transfers between devices with their start and end apart: 2, of which 2 were waited for; matrix products, arithmetic and copies ran while one was open for 0% of the time, Pallas kernels for 0%

profile of v1, /device:TPU:0, one launch (start us, length us, event | category | flops | bytes accessed | tf_op | source)
XLA Modules:
  0.0 285.9 jit_solution(13032438682829651300)
XLA Ops:
  8.2 16.3 %all_gather.9 = bf16[32,6144]{1,0:T(8,128)(2,1)S(1)} all-gather(bf16[8,6144]{1,0:T(8,128)(2,1)S(1)} %convert_element_type.12), channel_id=1, replica_groups=mesh['src'=8,'tgt'=4] {'tgt'}, dimensions={0}, use_global_device_ids=true | all-gather | bytes 491520 | tf_op jit(solution)/shard_map/all_gather | solution.py:21
  24.9 89.7 %while.22 = (s32[]{:T(128)}, f32[32,6144]{1,0:T(8,128)S(1)}, bf16[12,32,512]{2,1,0:T(8,128)(2,1)S(1)}, f32[12,3,512]{2,1,0:T(4,128)}, f32[3,6144]{1,0:T(4,128)}, /*index=5*/s32[]{:T(128)}, s32[]{:T(128)}, s32[]{}, s32[]{}) while((s32[]{:T(128)}, f32[32,6144]{1,0:T(8,128)S(1)}, bf16[12,32,512]{2,1,0:T(8,128)(2,1)S(1)}, ...), condition=%wide.region_1.2_spmd.clone, body=%wide.region_0.1_spmd.clone.sunk | while | flops 236322816 | bytes 1845391 | solution.py:29
  25.8 1.1 fusion.30
  26.9 5.5 %convolution_add_fusion.2 = f32[32,6144]{1,0:T(8,128)S(1)} fusion(f32[6144]{0:T(1024)S(1)} %bitcast.65, f32[512]{0:T(512)S(1)} %bitcast.72, f32[6144]{0:T(1024)S(1)} %bitcast.66, f32[512]{0:T(512)S(1)} %bitcast.71, f32[6144]{0:T(1024)S(1)} %bitcast.64, f32[512]{0:T(512)S(1)} %bitcast.70, f32[32,6144]{1,0:T(8,128)S(1)} %get-tuple-element.211, ...), kind=kOutput, calls=%fused_computation.10.clone.1 | convolution fusion | flops 236322816 | bytes 1685509 | tf_op jit(solution)/shard_map/while/body/eval_jaxpr/dot_general | solution.py:27
  34.4 5.5 %convolution_add_fusion.2 = f32[32,6144]{1,0:T(8,128)S(1)} fusion(f32[6144]{0:T(1024)S(1)} %bitcast.65, f32[512]{0:T(512)S(1)} %bitcast.72, f32[6144]{0:T(1024)S(1)} %bitcast.66, f32[512]{0:T(512)S(1)} %bitcast.71, f32[6144]{0:T(1024)S(1)} %bitcast.64, f32[512]{0:T(512)S(1)} %bitcast.70, f32[32,6144]{1,0:T(8,128)S(1)} %get-tuple-element.211, ...), kind=kOutput, calls=%fused_computation.10.clone.1 | convolution fusion | flops 236322816 | bytes 1685509 | tf_op jit(solution)/shard_map/while/body/eval_jaxpr/dot_general | solution.py:27
  41.8 5.5 %convolution_add_fusion.2 = f32[32,6144]{1,0:T(8,128)S(1)} fusion(f32[6144]{0:T(1024)S(1)} %bitcast.65, f32[512]{0:T(512)S(1)} %bitcast.72, f32[6144]{0:T(1024)S(1)} %bitcast.66, f32[512]{0:T(512)S(1)} %bitcast.71, f32[6144]{0:T(1024)S(1)} %bitcast.64, f32[512]{0:T(512)S(1)} %bitcast.70, f32[32,6144]{1,0:T(8,128)S(1)} %get-tuple-element.211, ...), kind=kOutput, calls=%fused_computation.10.clone.1 | convolution fusion | flops 236322816 | bytes 1685509 | tf_op jit(solution)/shard_map/while/body/eval_jaxpr/dot_general | solution.py:27
  49.3 5.5 %convolution_add_fusion.2 = f32[32,6144]{1,0:T(8,128)S(1)} fusion(f32[6144]{0:T(1024)S(1)} %bitcast.65, f32[512]{0:T(512)S(1)} %bitcast.72, f32[6144]{0:T(1024)S(1)} %bitcast.66, f32[512]{0:T(512)S(1)} %bitcast.71, f32[6144]{0:T(1024)S(1)} %bitcast.64, f32[512]{0:T(512)S(1)} %bitcast.70, f32[32,6144]{1,0:T(8,128)S(1)} %get-tuple-element.211, ...), kind=kOutput, calls=%fused_computation.10.clone.1 | convolution fusion | flops 236322816 | bytes 1685509 | tf_op jit(solution)/shard_map/while/body/eval_jaxpr/dot_general | solution.py:27
  56.8 5.5 %convolution_add_fusion.2 = f32[32,6144]{1,0:T(8,128)S(1)} fusion(f32[6144]{0:T(1024)S(1)} %bitcast.65, f32[512]{0:T(512)S(1)} %bitcast.72, f32[6144]{0:T(1024)S(1)} %bitcast.66, f32[512]{0:T(512)S(1)} %bitcast.71, f32[6144]{0:T(1024)S(1)} %bitcast.64, f32[512]{0:T(512)S(1)} %bitcast.70, f32[32,6144]{1,0:T(8,128)S(1)} %get-tuple-element.211, ...), kind=kOutput, calls=%fused_computation.10.clone.1 | convolution fusion | flops 236322816 | bytes 1685509 | tf_op jit(solution)/shard_map/while/body/eval_jaxpr/dot_general | solution.py:27
  64.3 5.5 %convolution_add_fusion.2 = f32[32,6144]{1,0:T(8,128)S(1)} fusion(f32[6144]{0:T(1024)S(1)} %bitcast.65, f32[512]{0:T(512)S(1)} %bitcast.72, f32[6144]{0:T(1024)S(1)} %bitcast.66, f32[512]{0:T(512)S(1)} %bitcast.71, f32[6144]{0:T(1024)S(1)} %bitcast.64, f32[512]{0:T(512)S(1)} %bitcast.70, f32[32,6144]{1,0:T(8,128)S(1)} %get-tuple-element.211, ...), kind=kOutput, calls=%fused_computation.10.clone.1 | convolution fusion | flops 236322816 | bytes 1685509 | tf_op jit(solution)/shard_map/while/body/eval_jaxpr/dot_general | solution.py:27
  71.7 5.5 %convolution_add_fusion.2 = f32[32,6144]{1,0:T(8,128)S(1)} fusion(f32[6144]{0:T(1024)S(1)} %bitcast.65, f32[512]{0:T(512)S(1)} %bitcast.72, f32[6144]{0:T(1024)S(1)} %bitcast.66, f32[512]{0:T(512)S(1)} %bitcast.71, f32[6144]{0:T(1024)S(1)} %bitcast.64, f32[512]{0:T(512)S(1)} %bitcast.70, f32[32,6144]{1,0:T(8,128)S(1)} %get-tuple-element.211, ...), kind=kOutput, calls=%fused_computation.10.clone.1 | convolution fusion | flops 236322816 | bytes 1685509 | tf_op jit(solution)/shard_map/while/body/eval_jaxpr/dot_general | solution.py:27
  79.2 5.5 %convolution_add_fusion.2 = f32[32,6144]{1,0:T(8,128)S(1)} fusion(f32[6144]{0:T(1024)S(1)} %bitcast.65, f32[512]{0:T(512)S(1)} %bitcast.72, f32[6144]{0:T(1024)S(1)} %bitcast.66, f32[512]{0:T(512)S(1)} %bitcast.71, f32[6144]{0:T(1024)S(1)} %bitcast.64, f32[512]{0:T(512)S(1)} %bitcast.70, f32[32,6144]{1,0:T(8,128)S(1)} %get-tuple-element.211, ...), kind=kOutput, calls=%fused_computation.10.clone.1 | convolution fusion | flops 236322816 | bytes 1685509 | tf_op jit(solution)/shard_map/while/body/eval_jaxpr/dot_general | solution.py:27
  86.7 5.5 %convolution_add_fusion.2 = f32[32,6144]{1,0:T(8,128)S(1)} fusion(f32[6144]{0:T(1024)S(1)} %bitcast.65, f32[512]{0:T(512)S(1)} %bitcast.72, f32[6144]{0:T(1024)S(1)} %bitcast.66, f32[512]{0:T(512)S(1)} %bitcast.71, f32[6144]{0:T(1024)S(1)} %bitcast.64, f32[512]{0:T(512)S(1)} %bitcast.70, f32[32,6144]{1,0:T(8,128)S(1)} %get-tuple-element.211, ...), kind=kOutput, calls=%fused_computation.10.clone.1 | convolution fusion | flops 236322816 | bytes 1685509 | tf_op jit(solution)/shard_map/while/body/eval_jaxpr/dot_general | solution.py:27
  94.1 5.5 %convolution_add_fusion.2 = f32[32,6144]{1,0:T(8,128)S(1)} fusion(f32[6144]{0:T(1024)S(1)} %bitcast.65, f32[512]{0:T(512)S(1)} %bitcast.72, f32[6144]{0:T(1024)S(1)} %bitcast.66, f32[512]{0:T(512)S(1)} %bitcast.71, f32[6144]{0:T(1024)S(1)} %bitcast.64, f32[512]{0:T(512)S(1)} %bitcast.70, f32[32,6144]{1,0:T(8,128)S(1)} %get-tuple-element.211, ...), kind=kOutput, calls=%fused_computation.10.clone.1 | convolution fusion | flops 236322816 | bytes 1685509 | tf_op jit(solution)/shard_map/while/body/eval_jaxpr/dot_general | solution.py:27
  101.6 5.5 %convolution_add_fusion.2 = f32[32,6144]{1,0:T(8,128)S(1)} fusion(f32[6144]{0:T(1024)S(1)} %bitcast.65, f32[512]{0:T(512)S(1)} %bitcast.72, f32[6144]{0:T(1024)S(1)} %bitcast.66, f32[512]{0:T(512)S(1)} %bitcast.71, f32[6144]{0:T(1024)S(1)} %bitcast.64, f32[512]{0:T(512)S(1)} %bitcast.70, f32[32,6144]{1,0:T(8,128)S(1)} %get-tuple-element.211, ...), kind=kOutput, calls=%fused_computation.10.clone.1 | convolution fusion | flops 236322816 | bytes 1685509 | tf_op jit(solution)/shard_map/while/body/eval_jaxpr/dot_general | solution.py:27
  109.1 5.5 %convolution_add_fusion.2 = f32[32,6144]{1,0:T(8,128)S(1)} fusion(f32[6144]{0:T(1024)S(1)} %bitcast.65, f32[512]{0:T(512)S(1)} %bitcast.72, f32[6144]{0:T(1024)S(1)} %bitcast.66, f32[512]{0:T(512)S(1)} %bitcast.71, f32[6144]{0:T(1024)S(1)} %bitcast.64, f32[512]{0:T(512)S(1)} %bitcast.70, f32[32,6144]{1,0:T(8,128)S(1)} %get-tuple-element.211, ...), kind=kOutput, calls=%fused_computation.10.clone.1 | convolution fusion | flops 236322816 | bytes 1685509 | tf_op jit(solution)/shard_map/while/body/eval_jaxpr/dot_general | solution.py:27
  115.8 47.1 %all-gather.3.cloned.1.call-done = f32[256,6144]{1,0:T(8,128)} async-done(((f32[32,6144]{1,0:T(8,128)}), f32[256,6144]{1,0:T(8,128)}) %all-gather.3.cloned.1.call-update) | async-done | bytes 6291472 | tf_op jit(solution)/shard_map/all_gather | solution.py:34
  162.9 3.2 %reduce_sum.9 = f32[32,6144]{1,0:T(8,128)S(1)} reduce(f32[8,32,6144]{2,1,0:T(8,128)} %bitcast.60, f32[]{:T(128)} %constant.25.clone.1), dimensions={0}, to_apply=%region_2.3 | reduce | flops 1376256 | bytes 7077892 | tf_op jit(solution)/shard_map/reduce_sum | solution.py:35
  166.9 86.2 %while.21 = (s32[]{:T(128)}, f32[12,32,512]{2,1,0:T(8,128)S(1)}, f32[12,3,512]{2,1,0:T(4,128)}, f32[3,6144]{1,0:T(4,128)S(1)}, bf16[32,6144]{1,0:T(8,128)(2,1)}, /*index=5*/s32[]{:T(128)}, s32[]{:T(128)}, s32[]{}, s32[]{}) while((s32[]{:T(128)}, f32[12,32,512]{2,1,0:T(8,128)S(1)}, f32[12,3,512]{2,1,0:T(4,128)}, f32[3,6144]{1,0:T(4,128)S(1)}, ...), condition=%wide.region_4.5_spmd, body=%wide.region_3.4_spmd.sunk | while | flops 235929600 | bytes 698501 | solution.py:46
  167.8 6.3 %fusion.28 = f32[12,32,512]{2,1,0:T(8,128)S(1)} fusion(f32[12,32,512]{2,1,0:T(8,128)S(1)} %get-tuple-element.238, s32[]{:T(128)} %get-tuple-element.237, bf16[32,6144]{1,0:T(8,128)(2,1)} %get-tuple-element.250, f32[6144]{0:T(1024)S(1)} %bitcast.68, f32[512]{0:T(512)S(1)} %bitcast.75, f32[6144]{0:T(1024)S(1)} %bitcast.69, f32[512]{0:T(512)S(1)} %bitcast.74, ...), kind=kOutput, calls=%fused_computation.3.clone.1 | convolution fusion | flops 235929600 | bytes 538628 | tf_op jit(solution)/shard_map/while/body/eval_jaxpr/dot_general | solution.py:44
  175.0 6.3 %fusion.28 = f32[12,32,512]{2,1,0:T(8,128)S(1)} fusion(f32[12,32,512]{2,1,0:T(8,128)S(1)} %get-tuple-element.238, s32[]{:T(128)} %get-tuple-element.237, bf16[32,6144]{1,0:T(8,128)(2,1)} %get-tuple-element.250, f32[6144]{0:T(1024)S(1)} %bitcast.68, f32[512]{0:T(512)S(1)} %bitcast.75, f32[6144]{0:T(1024)S(1)} %bitcast.69, f32[512]{0:T(512)S(1)} %bitcast.74, ...), kind=kOutput, calls=%fused_computation.3.clone.1 | convolution fusion | flops 235929600 | bytes 538628 | tf_op jit(solution)/shard_map/while/body/eval_jaxpr/dot_general | solution.py:44
  182.1 6.3 %fusion.28 = f32[12,32,512]{2,1,0:T(8,128)S(1)} fusion(f32[12,32,512]{2,1,0:T(8,128)S(1)} %get-tuple-element.238, s32[]{:T(128)} %get-tuple-element.237, bf16[32,6144]{1,0:T(8,128)(2,1)} %get-tuple-element.250, f32[6144]{0:T(1024)S(1)} %bitcast.68, f32[512]{0:T(512)S(1)} %bitcast.75, f32[6144]{0:T(1024)S(1)} %bitcast.69, f32[512]{0:T(512)S(1)} %bitcast.74, ...), kind=kOutput, calls=%fused_computation.3.clone.1 | convolution fusion | flops 235929600 | bytes 538628 | tf_op jit(solution)/shard_map/while/body/eval_jaxpr/dot_general | solution.py:44
  189.3 6.3 %fusion.28 = f32[12,32,512]{2,1,0:T(8,128)S(1)} fusion(f32[12,32,512]{2,1,0:T(8,128)S(1)} %get-tuple-element.238, s32[]{:T(128)} %get-tuple-element.237, bf16[32,6144]{1,0:T(8,128)(2,1)} %get-tuple-element.250, f32[6144]{0:T(1024)S(1)} %bitcast.68, f32[512]{0:T(512)S(1)} %bitcast.75, f32[6144]{0:T(1024)S(1)} %bitcast.69, f32[512]{0:T(512)S(1)} %bitcast.74, ...), kind=kOutput, calls=%fused_computation.3.clone.1 | convolution fusion | flops 235929600 | bytes 538628 | tf_op jit(solution)/shard_map/while/body/eval_jaxpr/dot_general | solution.py:44
  196.5 6.3 %fusion.28 = f32[12,32,512]{2,1,0:T(8,128)S(1)} fusion(f32[12,32,512]{2,1,0:T(8,128)S(1)} %get-tuple-element.238, s32[]{:T(128)} %get-tuple-element.237, bf16[32,6144]{1,0:T(8,128)(2,1)} %get-tuple-element.250, f32[6144]{0:T(1024)S(1)} %bitcast.68, f32[512]{0:T(512)S(1)} %bitcast.75, f32[6144]{0:T(1024)S(1)} %bitcast.69, f32[512]{0:T(512)S(1)} %bitcast.74, ...), kind=kOutput, calls=%fused_computation.3.clone.1 | convolution fusion | flops 235929600 | bytes 538628 | tf_op jit(solution)/shard_map/while/body/eval_jaxpr/dot_general | solution.py:44
  203.7 6.3 %fusion.28 = f32[12,32,512]{2,1,0:T(8,128)S(1)} fusion(f32[12,32,512]{2,1,0:T(8,128)S(1)} %get-tuple-element.238, s32[]{:T(128)} %get-tuple-element.237, bf16[32,6144]{1,0:T(8,128)(2,1)} %get-tuple-element.250, f32[6144]{0:T(1024)S(1)} %bitcast.68, f32[512]{0:T(512)S(1)} %bitcast.75, f32[6144]{0:T(1024)S(1)} %bitcast.69, f32[512]{0:T(512)S(1)} %bitcast.74, ...), kind=kOutput, calls=%fused_computation.3.clone.1 | convolution fusion | flops 235929600 | bytes 538628 | tf_op jit(solution)/shard_map/while/body/eval_jaxpr/dot_general | solution.py:44
  210.9 6.3 %fusion.28 = f32[12,32,512]{2,1,0:T(8,128)S(1)} fusion(f32[12,32,512]{2,1,0:T(8,128)S(1)} %get-tuple-element.238, s32[]{:T(128)} %get-tuple-element.237, bf16[32,6144]{1,0:T(8,128)(2,1)} %get-tuple-element.250, f32[6144]{0:T(1024)S(1)} %bitcast.68, f32[512]{0:T(512)S(1)} %bitcast.75, f32[6144]{0:T(1024)S(1)} %bitcast.69, f32[512]{0:T(512)S(1)} %bitcast.74, ...), kind=kOutput, calls=%fused_computation.3.clone.1 | convolution fusion | flops 235929600 | bytes 538628 | tf_op jit(solution)/shard_map/while/body/eval_jaxpr/dot_general | solution.py:44
  218.1 6.3 %fusion.28 = f32[12,32,512]{2,1,0:T(8,128)S(1)} fusion(f32[12,32,512]{2,1,0:T(8,128)S(1)} %get-tuple-element.238, s32[]{:T(128)} %get-tuple-element.237, bf16[32,6144]{1,0:T(8,128)(2,1)} %get-tuple-element.250, f32[6144]{0:T(1024)S(1)} %bitcast.68, f32[512]{0:T(512)S(1)} %bitcast.75, f32[6144]{0:T(1024)S(1)} %bitcast.69, f32[512]{0:T(512)S(1)} %bitcast.74, ...), kind=kOutput, calls=%fused_computation.3.clone.1 | convolution fusion | flops 235929600 | bytes 538628 | tf_op jit(solution)/shard_map/while/body/eval_jaxpr/dot_general | solution.py:44
  225.3 6.3 %fusion.28 = f32[12,32,512]{2,1,0:T(8,128)S(1)} fusion(f32[12,32,512]{2,1,0:T(8,128)S(1)} %get-tuple-element.238, s32[]{:T(128)} %get-tuple-element.237, bf16[32,6144]{1,0:T(8,128)(2,1)} %get-tuple-element.250, f32[6144]{0:T(1024)S(1)} %bitcast.68, f32[512]{0:T(512)S(1)} %bitcast.75, f32[6144]{0:T(1024)S(1)} %bitcast.69, f32[512]{0:T(512)S(1)} %bitcast.74, ...), kind=kOutput, calls=%fused_computation.3.clone.1 | convolution fusion | flops 235929600 | bytes 538628 | tf_op jit(solution)/shard_map/while/body/eval_jaxpr/dot_general | solution.py:44
  232.4 6.3 %fusion.28 = f32[12,32,512]{2,1,0:T(8,128)S(1)} fusion(f32[12,32,512]{2,1,0:T(8,128)S(1)} %get-tuple-element.238, s32[]{:T(128)} %get-tuple-element.237, bf16[32,6144]{1,0:T(8,128)(2,1)} %get-tuple-element.250, f32[6144]{0:T(1024)S(1)} %bitcast.68, f32[512]{0:T(512)S(1)} %bitcast.75, f32[6144]{0:T(1024)S(1)} %bitcast.69, f32[512]{0:T(512)S(1)} %bitcast.74, ...), kind=kOutput, calls=%fused_computation.3.clone.1 | convolution fusion | flops 235929600 | bytes 538628 | tf_op jit(solution)/shard_map/while/body/eval_jaxpr/dot_general | solution.py:44
  239.6 6.3 %fusion.28 = f32[12,32,512]{2,1,0:T(8,128)S(1)} fusion(f32[12,32,512]{2,1,0:T(8,128)S(1)} %get-tuple-element.238, s32[]{:T(128)} %get-tuple-element.237, bf16[32,6144]{1,0:T(8,128)(2,1)} %get-tuple-element.250, f32[6144]{0:T(1024)S(1)} %bitcast.68, f32[512]{0:T(512)S(1)} %bitcast.75, f32[6144]{0:T(1024)S(1)} %bitcast.69, f32[512]{0:T(512)S(1)} %bitcast.74, ...), kind=kOutput, calls=%fused_computation.3.clone.1 | convolution fusion | flops 235929600 | bytes 538628 | tf_op jit(solution)/shard_map/while/body/eval_jaxpr/dot_general | solution.py:44
  246.8 6.3 %fusion.28 = f32[12,32,512]{2,1,0:T(8,128)S(1)} fusion(f32[12,32,512]{2,1,0:T(8,128)S(1)} %get-tuple-element.238, s32[]{:T(128)} %get-tuple-element.237, bf16[32,6144]{1,0:T(8,128)(2,1)} %get-tuple-element.250, f32[6144]{0:T(1024)S(1)} %bitcast.68, f32[512]{0:T(512)S(1)} %bitcast.75, f32[6144]{0:T(1024)S(1)} %bitcast.69, f32[512]{0:T(512)S(1)} %bitcast.74, ...), kind=kOutput, calls=%fused_computation.3.clone.1 | convolution fusion | flops 235929600 | bytes 538628 | tf_op jit(solution)/shard_map/while/body/eval_jaxpr/dot_general | solution.py:44
  254.8 22.7 %reduce-scatter.2.cloned.1.call-done = f32[8,6144]{1,0:T(8,128)} async-done(((f32[32,6144]{1,0:T(8,128)}), f32[8,6144]{1,0:T(8,128)}) %reduce-scatter.2.cloned.1.call-update) | async-done | bytes 196624 | tf_op jit(solution)/shard_map/reduce_scatter | solution.py:48
  277.4 1.6 multiply_divide_fusion.1
  (67 shorter events, 37.7 us)
Async XLA Ops:
  7.2 155.7 %all-gather.3.cloned.1.call-start = ((), (), s32[]{:S(2)}) async-start(), calls=%async_computation.2 | async-start | bytes 7077888 | tf_op jit(solution)/shard_map/all_gather | solution.py:34
  114.6 0.9 copy-start.1
  114.6 51.4 %copy-start.2 = (f32[32,6144]{1,0:T(8,128)S(1)}, f32[32,6144]{1,0:T(8,128)}, u32[]{:S(2)}) copy-start(f32[32,6144]{1,0:T(8,128)} %param.13) | copy-start | bytes 2359300
  114.6 52.3 %copy-start = (f32[3,6144]{1,0:T(4,128)S(1)}, f32[3,6144]{1,0:T(4,128)}, u32[]{:S(2)}) copy-start(f32[3,6144]{1,0:T(4,128)} %get-tuple-element.258) | copy-start | bytes 221188
  115.6 161.9 %reduce-scatter.2.cloned.1.call-start = ((), (), s32[]{:S(2)}) async-start(), calls=%async_computation.1 | async-start | bytes 983040 | tf_op jit(solution)/shard_map/reduce_scatter | solution.py:48
  166.9 110.5 %copy-start.3 = (f32[8,6144]{1,0:T(8,128)S(1)}, f32[8,6144]{1,0:T(8,128)}, u32[]{:S(2)}) copy-start(f32[8,6144]{1,0:T(8,128)} %param.12) | copy-start | bytes 589828
Sparse Core Ops, SparseCore 0:
  115.7 47.1 all-gather.2
  254.2 23.1 reduce-scatter.1
